TPU v7x, 32 devices: a whole 2x2x4 slice. The times are simulated.
32 devices in a mesh: tok: 8 (over z, y), head: 4 (over x, core).
Axes of the slice: x: 2, y: 2, z: 4, core: 2. Of those that a mesh axis runs over, the one named last changes fastest.
Arguments:
- queries: bfloat16 [8192, 4096], P(('tok', 'head')), may hold values from -64 to 64
- keys: bfloat16 [8192, 4096], P(('tok', 'head')), may hold values from -6 to 6
- values: bfloat16 [8192, 4096], P(('tok', 'head')), may hold values from -6 to 6
- token_rates: bfloat16 [8192, 8], P(('tok', 'head')), may hold values from 0.099609375 to 1
- gate_start: bfloat16 [8, 512, 1024], P('head'), may hold values from -0.25 to 0.25
- up_start: bfloat16 [8, 512, 1024], P('head'), may hold values from -0.25 to 0.25
- down_start: bfloat16 [8, 1024, 512], P('head'), may hold values from -0.1875 to 0.1875
- norm_gain: float32 [4096], replicated, may hold values from 0.25 to 1.75
- bounds: int32 [4], replicated, may hold values from 896 to 1152
Outputs:
- layer_out: bfloat16 [8192, 4096], P(('tok', 'head'))
Inputs may be any that keep to these rules, and one draw needn't show every extreme that they name: The first span of segment s is its positions below bounds[s].
All inputs are finite; a program needn't handle non-finite values.
Results may differ from a plain program's by a relative error of at most 0.02.
Values may be sent and summed in bfloat16 or wider, within the bound.
A program may use at most 192 MiB of HBM per device.

v0:
```python
import math

import jax
import jax.numpy as jnp
from jax import lax
from jax.sharding import PartitionSpec as P

FDIM = 512
AHD = 128
WINDOW = 512
NS_ITERS = 3


linear_coef = 3.4445
cubic_coef = -4.775
quintic_coef = 2.0315
update_step = 1.0
rms_epsilon = 1e-05
norm_epsilon = 1e-06


def swapped(value, axis, apart):
    return lax.ppermute(value, axis, [(i, i ^ 1 << apart) for i in range(lax.axis_size(axis))])


def shifted(value, axis, steps):
    count = lax.axis_size(axis)
    first, last = (max(0, -steps), min(count, count - steps))
    return lax.ppermute(value, axis, [(source, source + steps) for source in range(first, last)])


def silu_slope(pre_act):
    logistic = jax.nn.sigmoid(pre_act)
    return logistic * (1.0 + pre_act * (1.0 - logistic))


def orthogonal(gradient):
    frob_norm = jnp.sqrt(jnp.sum(gradient * gradient) + norm_epsilon)
    iterate = (gradient / frob_norm).astype(jnp.bfloat16)
    for sweep_index in range(NS_ITERS):
        gram_matrix = jnp.dot(iterate, iterate.T, preferred_element_type=jnp.float32).astype(
            jnp.bfloat16
        )
        gram_square = jnp.dot(gram_matrix, gram_matrix, preferred_element_type=jnp.float32)
        poly_mix = (
            cubic_coef * gram_matrix.astype(jnp.float32) + quintic_coef * gram_square
        ).astype(jnp.bfloat16)
        iterate = (
            linear_coef * iterate.astype(jnp.float32)
            + jnp.dot(poly_mix, iterate, preferred_element_type=jnp.float32)
        ).astype(jnp.bfloat16)
    return iterate.astype(jnp.float32)


def renorm(updated, w_start):
    start_wide = w_start.astype(jnp.float32)
    target = jnp.sqrt(jnp.sum(start_wide * start_wide, axis=0) + norm_epsilon)
    actual = jnp.sqrt(jnp.sum(updated * updated, axis=0) + norm_epsilon)
    return (updated * (target / actual)).astype(jnp.bfloat16)


def swiglu_apply(in_rows, w_gate, w_up, w_down):
    pre_gate = jnp.dot(in_rows, w_gate, preferred_element_type=jnp.float32)
    pre_up = jnp.dot(in_rows, w_up, preferred_element_type=jnp.float32)
    hidden = (jax.nn.silu(pre_gate) * pre_up).astype(jnp.bfloat16)
    return jnp.dot(hidden, w_down, preferred_element_type=jnp.float32)


def fast_item(q_item, k_item, v_item, rate_row, span_bound, w_gate, w_up, w_down, gain_head):
    length = q_item.shape[0]
    split_low = length // 2 - length // 16
    split_high = length // 2 + length // 16
    in_span = jnp.arange(split_high) < span_bound
    k_rows = k_item[:split_high]
    pre_gate = jnp.dot(k_rows, w_gate, preferred_element_type=jnp.float32)
    pre_up = jnp.dot(k_rows, w_up, preferred_element_type=jnp.float32)
    active = jax.nn.silu(pre_gate)
    hidden = (active * pre_up).astype(jnp.bfloat16)
    weighted = rate_row[:split_high].astype(jnp.float32)[:, None] * v_item[:split_high].astype(
        jnp.float32
    )
    target = jnp.where(in_span[:, None], weighted, 0.0).astype(jnp.bfloat16)
    grad_down = jnp.dot(hidden.T, target, preferred_element_type=jnp.float32)
    back_grad = jnp.dot(target, w_down.T, preferred_element_type=jnp.float32)
    d_gate = (back_grad * pre_up * silu_slope(pre_gate)).astype(jnp.bfloat16)
    d_up = (back_grad * active).astype(jnp.bfloat16)
    grad_gate = jnp.dot(k_rows.T, d_gate, preferred_element_type=jnp.float32)
    grad_up = jnp.dot(k_rows.T, d_up, preferred_element_type=jnp.float32)
    new_gate = renorm(w_gate.astype(jnp.float32) + update_step * orthogonal(grad_gate), w_gate)
    new_up = renorm(w_up.astype(jnp.float32) + update_step * orthogonal(grad_up), w_up)
    new_down = renorm(w_down.astype(jnp.float32) + update_step * orthogonal(grad_down.T).T, w_down)
    before_out = swiglu_apply(q_item[:split_high], w_gate, w_up, w_down)
    after_out = swiglu_apply(q_item[split_low:], new_gate, new_up, new_down)
    middle = jnp.where(
        (jnp.arange(split_low, split_high) < span_bound)[:, None],
        before_out[split_low:],
        after_out[: split_high - split_low],
    )
    combined = jnp.concatenate(
        [before_out[:split_low], middle, after_out[split_high - split_low :]], axis=0
    )
    root_mean = jnp.sqrt(jnp.mean(combined * combined, axis=-1, keepdims=True) + rms_epsilon)
    return (combined / root_mean * gain_head).astype(jnp.bfloat16)


def attend_rows(query_rows, key_rows, value_rows, query_place, key_place):
    query_count, feat_width = query_rows.shape
    head_count = feat_width // AHD
    q_heads = query_rows.reshape(query_count, head_count, AHD)
    k_heads = key_rows.reshape(key_rows.shape[0], head_count, AHD)
    v_heads = value_rows.reshape(value_rows.shape[0], head_count, AHD)
    scores = jnp.einsum(
        "qhd,khd->hqk", q_heads, k_heads, preferred_element_type=jnp.float32
    ) / math.sqrt(AHD)
    pos_gap = query_place[:, None] - key_place[None, :]
    allowed = ((pos_gap >= 0) & (pos_gap < WINDOW) & (key_place[None, :] >= 0))[None]
    masked = jnp.where(allowed, scores, -jnp.inf)
    row_max = jnp.max(masked, axis=-1, keepdims=True)
    weights = jnp.where(allowed, jnp.exp(masked - row_max), 0.0)
    row_total = jnp.sum(weights, axis=-1)
    mixed_out = jnp.einsum(
        "hqk,khd->qhd", weights.astype(jnp.bfloat16), v_heads, preferred_element_type=jnp.float32
    )
    return (
        (mixed_out / row_total.T[:, :, None]).reshape(query_count, feat_width).astype(jnp.bfloat16)
    )


def token_attention(queries, key_parts, value_parts, shard, reach, returned):
    row_count = queries.shape[0]
    key_rows = jnp.concatenate(key_parts, axis=0)
    value_rows = jnp.concatenate(value_parts, axis=0)
    query_place = shard * row_count + jnp.arange(row_count)
    key_place = (shard - reach) * row_count + jnp.arange(key_rows.shape[0])
    attn_rows = attend_rows(queries, key_rows, value_rows, query_place, key_place)
    return (attn_rows.astype(jnp.float32) + returned.astype(jnp.float32)).astype(jnp.bfloat16)


def column_half(block, which):
    half_width = block.shape[1] // 2
    return lax.dynamic_slice_in_dim(block, which * half_width, half_width, 1)


def order_rows(own_rows, other_rows, parity):
    return jnp.where(
        parity == 0,
        jnp.concatenate([own_rows, other_rows], axis=0),
        jnp.concatenate([other_rows, own_rows], axis=0),
    )


def body(queries, keys, values, token_rates, gate_start, up_start, down_start, norm_gain, bounds):
    row_count = queries.shape[0]
    group_count = lax.axis_size("head")
    shard = lax.axis_index(("tok", "head"))
    parity = lax.axis_index("tok") % 2
    column = lax.axis_index("head")
    owned = 2 * column + parity
    sequence = shard // (2 * group_count)
    other = 1 - parity
    spread_q, spread_k, spread_v, spread_r = (
        lax.all_to_all(queries, "head", split_axis=1, concat_axis=0, tiled=True),
        lax.all_to_all(keys, "head", split_axis=1, concat_axis=0, tiled=True),
        lax.all_to_all(values, "head", split_axis=1, concat_axis=0, tiled=True),
        lax.all_to_all(token_rates, "head", split_axis=1, concat_axis=0, tiled=True),
    )
    passed_q, passed_k, passed_v, passed_r = swapped(
        (
            column_half(spread_q, other),
            column_half(spread_k, other),
            column_half(spread_v, other),
            column_half(spread_r, other),
        ),
        "tok",
        0,
    )
    item_q = order_rows(column_half(spread_q, parity), passed_q, parity)
    item_k = order_rows(column_half(spread_k, parity), passed_k, parity)
    item_v = order_rows(column_half(spread_v, parity), passed_v, parity)
    item_r = order_rows(column_half(spread_r, parity), passed_r, parity)
    rate_row = item_r.reshape(-1)
    w_gate = lax.dynamic_index_in_dim(gate_start, parity, 0, keepdims=False)
    w_up = lax.dynamic_index_in_dim(up_start, parity, 0, keepdims=False)
    w_down = lax.dynamic_index_in_dim(down_start, parity, 0, keepdims=False)
    gain_head = lax.dynamic_slice_in_dim(norm_gain, owned * FDIM, FDIM, 0)
    span_bound = lax.dynamic_index_in_dim(bounds, sequence, 0, keepdims=False)
    carried = fast_item(
        item_q, item_k, item_v, rate_row, span_bound, w_gate, w_up, w_down, gain_head
    )
    halves = carried.reshape(2, -1, carried.shape[1])
    mine = lax.dynamic_index_in_dim(halves, parity, 0, keepdims=False)
    theirs = lax.dynamic_index_in_dim(halves, other, 0, keepdims=False)
    received = swapped(theirs, "tok", 0)
    paired = jnp.where(
        parity == 0,
        jnp.concatenate([mine, received], axis=1),
        jnp.concatenate([received, mine], axis=1),
    )
    returned = lax.all_to_all(paired, "head", split_axis=0, concat_axis=1, tiled=True)
    reach = (WINDOW + row_count - 1) // row_count
    carried_pair = (keys, values)
    key_parts = [keys]
    value_parts = [values]
    for distance in range(reach):
        carried_pair = shifted((carried_pair[0], carried_pair[1]), ("tok", "head"), 1)
        key_parts.insert(0, carried_pair[0])
        value_parts.insert(0, carried_pair[1])
    layer_out = token_attention(queries, key_parts, value_parts, shard, reach, returned)
    return layer_out


def solution(mesh):
    return jax.shard_map(
        body,
        mesh=mesh,
        in_specs=(
            P(("tok", "head"), None),
            P(("tok", "head"), None),
            P(("tok", "head"), None),
            P(("tok", "head"), None),
            P("head", None, None),
            P("head", None, None),
            P("head", None, None),
            P(),
            P(),
        ),
        out_specs=P(("tok", "head"), None),
        check_vma=False,
    )
```

profile of v0, /device:TPU:11, one launch (start us, length us, event | category | flops | bytes accessed | tf_op | source)
XLA Modules:
  0.0 450.6 jit_solution(10942575508436591151)
XLA Ops:
  18.1 19.8 %all-to-all-done.3 = bf16[256,4,1024]{0,2,1:T(8,128)(2,1)} async-done(((bf16[256,4,1024]{0,2,1:T(8,128)(2,1)}), bf16[256,4,1024]{0,2,1:T(8,128)(2,1)}, u32[]{:S(2)}, u32[]{:S(2)}) %all-to-all-start.3) | async-done | bytes 2097184 | tf_op jit(solution)/shard_map/all_to_all | solution.py:164
  37.9 6.3 %all-to-all-start.1 = ((bf16[256,4,1024]{0,2,1:T(8,128)(2,1)}), bf16[256,4,1024]{0,2,1:T(8,128)(2,1)}, u32[]{:S(2)}, u32[]{:S(2)}) async-start(bf16[256,4,1024]{0,2,1:T(8,128)(2,1)} %bitcast.137), calls=%async_computation.1 | async-start | bytes 4194304 | tf_op jit(solution)/shard_map/all_to_all | solution.py:163
  51.2 16.9 %all-to-all-done.1 = bf16[256,4,1024]{0,2,1:T(8,128)(2,1)} async-done(((bf16[256,4,1024]{0,2,1:T(8,128)(2,1)}), bf16[256,4,1024]{0,2,1:T(8,128)(2,1)}, u32[]{:S(2)}, u32[]{:S(2)}) %all-to-all-start.1) | async-done | bytes 2097184 | tf_op jit(solution)/shard_map/all_to_all | solution.py:163
  68.1 6.8 %all-to-all-start = ((bf16[256,4,1024]{0,2,1:T(8,128)(2,1)}), bf16[256,4,1024]{0,2,1:T(8,128)(2,1)}, u32[]{:S(2)}, u32[]{:S(2)}) async-start(bf16[256,4,1024]{0,2,1:T(8,128)(2,1)} %bitcast.142), calls=%async_computation | async-start | bytes 4194304 | tf_op jit(solution)/shard_map/all_to_all | solution.py:162
  81.9 23.1 %collective-permute-start.5 = (bf16[1024,512]{1,0:T(8,128)(2,1)}, bf16[1024,512]{1,0:T(8,128)(2,1)}, u32[]{:S(2)}, u32[]{:S(2)}) collective-permute-start(bf16[1024,512]{1,0:T(8,128)(2,1)} %get-tuple-element.20), channel_id=1, source_target_pairs={{0,4},{4,0},{8,12},{12,8},{16,20},{20,16},{24,28},{28,24},{1,5},{5... | collective-permute-start | bytes 3145736 | tf_op jit(solution)/shard_map/ppermute | solution.py:23
  118.8 32.3 %collective-permute-done.6 = bf16[1024,1]{0,1:T(2,128)(2,1)S(1)} collective-permute-done((bf16[1024,1]{0,1:T(2,128)(2,1)S(1)}, bf16[1024,1]{0,1:T(2,128)(2,1)S(1)}, u32[]{:S(2)}, u32[]{:S(2)}) %collective-permute-start.6) | collective-permute-done | bytes 2080 | tf_op jit(solution)/shard_map/ppermute | solution.py:23
  156.6 25.7 %collective-permute-start.3 = (bf16[256,4096]{0,1:T(8,128)(2,1)}, bf16[256,4096]{0,1:T(8,128)(2,1)}, u32[]{:S(2)}, u32[]{:S(2)}) collective-permute-start(bf16[256,4096]{0,1:T(8,128)(2,1)} %collective-permute-done.2), channel_id=1, source_target_pairs={{0,1},{1,2},{2,3},{3,4},{4,5},{5,6},{6,7},{7,8},{8,9},{9,10},{10,1... | collective-permute-start | bytes 6291464 | tf_op jit(solution)/shard_map/ppermute | solution.py:29
  185.5 4.7 %fusion.47 = f32[1152,1024]{1,0:T(8,128)S(1)} fusion(bf16[1,1024,512]{2,1,0:T(8,128)(2,1)S(1)} %copy-done.11, bf16[1024,512]{1,0:T(8,128)(2,1)} %collective-permute-done.7, bf16[1024,512]{1,0:T(8,128)(2,1)S(1)} %copy-done.13, f32[1152]{0:T(1024)S(1)} %fusion.121, pred[1152]{0:T(1024)(128)(4,1)S(1)} %iota_compare_fusion, pred[]{:T(512)S(6)} %eq.4), kind=kOutput, calls=%fused_computation.115 | convolution fusion | flops 1215627264 | bytes 7870081 | tf_op jit(solution)/shard_map/dot_general | solution.py:84
  213.8 6.7 %multiply_reduce_fusion.6 = (f32[]{:T(128)}, f32[512,1024]{1,0:T(8,128)}) fusion(bf16[1152,512]{1,0:T(8,128)(2,1)S(1)} %fusion.45, f32[1152,1024]{1,0:T(8,128)S(1)} %bitcast.146, f32[1152,1024]{1,0:T(8,128)} %copy-done.20, f32[1152,1024]{1,0:T(8,128)S(1)} %fusion.53), kind=kOutput, calls=%fused_computation.67 | convolution fusion | flops 1220804608 | bytes 17432580 | tf_op jit(solution)/shard_map/dot_general | solution.py:87
  253.1 4.8 %fusion.18 = (f32[1024]{0:T(1024)S(1)}, f32[1024]{0:T(1024)S(1)}, bf16[512,1024]{1,0:T(8,128)(2,1)}) fusion(bf16[2,512,1024]{2,1,0:T(8,128)(2,1)} %param.14, s32[]{:T(128)S(6)} %select_n.105, bf16[512,1024]{1,0:T(8,128)(2,1)} %add_convert_fusion.3, bf16[512,512]{1,0:T(8,128)(2,1)} %convolution_convert_fusion.3), kind=kOutput, calls=%fused_computation.39 | convolution fusion | flops 812382208 | bytes 5775364 | tf_op jit(solution)/shard_map/dot_general | solution.py:50
  268.2 7.0 %fusion.25 = f32[1152,512]{1,0:T(8,128)} fusion(f32[1152,1024]{1,0:T(8,128)} %fusion.60, bf16[1,1024,512]{2,1,0:T(8,128)(2,1)S(1)} %copy-done.12, bf16[2048,512]{1,0:T(8,128)(2,1)S(1)} %maximum_select_fusion, bf16[2,512,1024]{2,1,0:T(8,128)(2,1)} %param.14, s32[]{:T(128)S(6)} %select_n.105), kind=kOutput, calls=%fused_computation.69 | convolution fusion | flops 2422996992 | bytes 10354692 | tf_op jit(solution)/shard_map/dot_general | solution.py:66
  275.2 5.0 %fusion.19 = (f32[512]{0:T(512)S(1)}, f32[512]{0:T(512)S(1)}, bf16[1024,512]{0,1:T(8,128)(2,1)}) fusion(bf16[1,1024,512]{1,2,0:T(8,128)(2,1)} %copy.51, bf16[512,1024]{1,0:T(8,128)(2,1)} %copy-done.17, bf16[512,512]{1,0:T(8,128)(2,1)} %convolution_convert_fusion), kind=kOutput, calls=%fused_computation.40 | convolution fusion | flops 812383232 | bytes 3674112 | tf_op jit(solution)/shard_map/dot_general | solution.py:50
  280.3 5.2 %fusion.46 = f32[1152,1024]{1,0:T(8,128)} fusion(bf16[512,1024]{1,0:T(8,128)(2,1)} %get-tuple-element.25, f32[1024]{0:T(1024)S(1)} %rsqrt_multiply_fusion.1, bf16[2048,512]{1,0:T(8,128)(2,1)S(1)} %maximum_select_fusion, bf16[2,512,1024]{2,1,0:T(8,128)(2,1)} %param.13, s32[]{:T(128)S(6)} %select_n.105), kind=kOutput, calls=%fused_computation.114 | convolution fusion | flops 1210580992 | bytes 7999492 | tf_op jit(solution)/shard_map/dot_general | solution.py:63
  285.5 7.6 %fusion.24 = f32[1152,512]{1,0:T(8,128)} fusion(f32[1152,1024]{1,0:T(8,128)} %fusion.46, bf16[512,1024]{1,0:T(8,128)(2,1)} %get-tuple-element.31, bf16[1024,512]{0,1:T(8,128)(2,1)} %get-tuple-element.30, bf16[1,1024,512]{1,2,0:T(8,128)(2,1)S(1)} %copy-done.15, f32[512]{0:T(512)S(1)} %rsqrt_multiply_fusion.2, f32[1024]{0:T(1024)S(1)} %rsqrt_multiply_fusion, ...), kind=kOutput, calls=%fused_computation.68 | convolution fusion | flops 2428239872 | bytes 12457988 | tf_op jit(solution)/shard_map/dot_general | solution.py:66
  307.3 10.6 %collective-permute-done.8 = bf16[1024,512]{1,0:T(8,128)(2,1)S(1)} collective-permute-done((bf16[1024,512]{1,0:T(8,128)(2,1)}, bf16[1024,512]{1,0:T(8,128)(2,1)S(1)}, u32[]{:S(2)}, u32[]{:S(2)}) %collective-permute-start.8) | collective-permute-done | bytes 1048608 | tf_op jit(solution)/shard_map/ppermute | solution.py:23
  319.9 36.9 %all-to-all-start.4 = ((bf16[4,256,1024]{2,1,0:T(8,128)(2,1)}), bf16[4,256,1024]{2,1,0:T(8,128)(2,1)}, u32[]{:S(2)}, u32[]{:S(2)}) async-start(bf16[4,256,1024]{2,1,0:T(8,128)(2,1)} %maximum_select_fusion.1), calls=%async_computation.4 | async-start | bytes 4194304 | tf_op jit(solution)/shard_map/all_to_all | solution.py:199
  356.8 5.4 %pad_maximum_fusion.1 = bf16[768,4096]{0,1:T(8,128)(2,1)} fusion(bf16[256,4096]{0,1:T(8,128)(2,1)S(1)} %copy-done.2, bf16[256,4096]{0,1:T(8,128)(2,1)} %collective-permute-done.2, bf16[256,4096]{0,1:T(8,128)(2,1)} %collective-permute-done.3), kind=kLoop, calls=%fused_computation.10 | loop fusion | flops 18874368 | bytes 12582912 | tf_op jit(solution)/shard_map/concatenate | solution.py:131
  362.2 15.2 %fusion.20 = f32[32,768,256]{2,1,0:T(8,128)} fusion(bf16[768,32,128]{0,2,1:T(8,128)(2,1)} %bitcast.136, bf16[256,4096]{1,0:T(8,128)(2,1)} %param.9), kind=kOutput, calls=%fused_computation.41 | convolution fusion | flops 1610612736 | bytes 33554432 | tf_op jit(solution)/shard_map/qhd,khd->hqk/dot_general | solution.py:112
  377.4 30.0 %fusion.155 = (f32[32,256]{1,0:T(8,128)S(1)}, bf16[32,256,768]{1,2,0:T(8,128)(2,1)}) fusion(f32[32,768,256]{2,1,0:T(8,128)} %fusion.20, pred[256,768]{0,1:T(8,128)(4,1)S(1)} %fusion.93), kind=kOutput, calls=%fused_computation.236 | output fusion | flops 50332416 | bytes 37978112 | tf_op jit(solution)/shard_map/sub | solution.py:119
  407.3 6.4 %pad_maximum_fusion = bf16[768,4096]{1,0:T(8,128)(2,1)} fusion(bf16[256,4096]{1,0:T(8,128)(2,1)} %param.11, bf16[256,4096]{1,0:T(8,128)(2,1)} %collective-permute-done, bf16[256,4096]{1,0:T(8,128)(2,1)} %collective-permute-done.1), kind=kLoop, calls=%fused_computation.9 | loop fusion | flops 18874368 | bytes 12582912 | tf_op jit(solution)/shard_map/concatenate | solution.py:132
  413.7 8.6 %copy.43 = bf16[768,4096]{0,1:T(8,128)(2,1)} copy(bf16[768,4096]{1,0:T(8,128)(2,1)} %pad_maximum_fusion) | data formatting | bytes 12582912 | tf_op jit(solution)/shard_map/concatenate | solution.py:132
  422.3 9.5 %fusion.9 = bf16[256,32,128]{0,2,1:T(8,128)(2,1)} fusion(bf16[768,32,128]{0,2,1:T(8,128)(2,1)} %bitcast.144, bf16[32,256,768]{1,2,0:T(8,128)(2,1)} %get-tuple-element.33, f32[256,32]{0,1:T(8,128)S(1)} %bitcast.150), kind=kOutput, calls=%fused_computation.22 | convolution fusion | flops 1612709888 | bytes 21004288 | tf_op jit(solution)/shard_map/hqk,khd->qhd/dot_general | solution.py:121
  435.9 5.4 %copy.57 = f32[256,4,1024]{0,2,1:T(8,128)} copy(f32[256,4,1024]{2,0,1:T(8,128)} %convert_bitcast_fusion) | data formatting | bytes 8388608 | tf_op jit(solution)/shard_map/convert_element_type | solution.py:136
  441.3 4.8 %fusion.8 = bf16[256,4096]{0,1:T(8,128)(2,1)} fusion(f32[256,4,1024]{0,2,1:T(8,128)} %copy.57, bf16[256,32,128]{0,2,1:T(8,128)(2,1)} %fusion.9), kind=kLoop, calls=%fused_computation.20 | loop fusion | flops 3145728 | bytes 8388608 | tf_op jit(solution)/shard_map/convert_element_type | solution.py:136
  (129 shorter events, 142.9 us)
Async XLA Ops:
  0.0 107.7 %copy-start = (bf16[2,1024,512]{2,1,0:T(8,128)(2,1)S(1)}, bf16[2,1024,512]{2,1,0:T(8,128)(2,1)}, u32[]{:S(2)}) copy-start(bf16[2,1024,512]{2,1,0:T(8,128)(2,1)} %param.15) | copy-start | bytes 6291460
  1.4 8.1 %all-to-all-start.2 = ((bf16[256,4,2]{0,2,1:T(2,128)(2,1)}), bf16[256,4,2]{0,2,1:T(2,128)(2,1)S(1)}, u32[]{:S(2)}, u32[]{:S(2)}) async-start(bf16[256,4,2]{0,2,1:T(2,128)(2,1)} %all_to_all.72), calls=%async_computation.2 | async-start | bytes 8192 | tf_op jit(solution)/shard_map/all_to_all | solution.py:165
  9.6 28.4 %all-to-all-start.3 = ((bf16[256,4,1024]{0,2,1:T(8,128)(2,1)}), bf16[256,4,1024]{0,2,1:T(8,128)(2,1)}, u32[]{:S(2)}, u32[]{:S(2)}) async-start(bf16[256,4,1024]{0,2,1:T(8,128)(2,1)} %bitcast.143), calls=%async_computation.3 | async-start | bytes 4194304 | tf_op jit(solution)/shard_map/all_to_all | solution.py:164
  37.9 30.2 %all-to-all-start.1 = ((bf16[256,4,1024]{0,2,1:T(8,128)(2,1)}), bf16[256,4,1024]{0,2,1:T(8,128)(2,1)}, u32[]{:S(2)}, u32[]{:S(2)}) async-start(bf16[256,4,1024]{0,2,1:T(8,128)(2,1)} %bitcast.137), calls=%async_computation.1 | async-start | bytes 4194304 | tf_op jit(solution)/shard_map/all_to_all | solution.py:163
  44.2 112.4 %collective-permute-start.2 = (bf16[256,4096]{0,1:T(8,128)(2,1)}, bf16[256,4096]{0,1:T(8,128)(2,1)}, u32[]{:S(2)}, u32[]{:S(2)}) collective-permute-start(bf16[256,4096]{0,1:T(8,128)(2,1)} %copy.44), channel_id=1, source_target_pairs={{0,1},{1,2},{2,3},{3,4},{4,5},{5,6},{6,7},{7,8},{8,9},{9,10},{10,1... | collective-permute-start | bytes 6291464 | tf_op jit(solution)/shard_map/ppermute | solution.py:29
  68.1 83.0 %all-to-all-start = ((bf16[256,4,1024]{0,2,1:T(8,128)(2,1)}), bf16[256,4,1024]{0,2,1:T(8,128)(2,1)}, u32[]{:S(2)}, u32[]{:S(2)}) async-start(bf16[256,4,1024]{0,2,1:T(8,128)(2,1)} %bitcast.142), calls=%async_computation | async-start | bytes 4194304 | tf_op jit(solution)/shard_map/all_to_all | solution.py:162
  79.0 28.1 %copy-start.16 = (s32[4]{0:T(128)S(1)}, s32[4]{0:T(128)}, u32[]{:S(2)}) copy-start(s32[4]{0:T(128)} %param.17) | copy-start | bytes 52
  81.9 100.3 %collective-permute-start.5 = (bf16[1024,512]{1,0:T(8,128)(2,1)}, bf16[1024,512]{1,0:T(8,128)(2,1)}, u32[]{:S(2)}, u32[]{:S(2)}) collective-permute-start(bf16[1024,512]{1,0:T(8,128)(2,1)} %get-tuple-element.20), channel_id=1, source_target_pairs={{0,4},{4,0},{8,12},{12,8},{16,20},{20,16},{24,28},{28,24},{1,5},{5... | collective-permute-start | bytes 3145736 | tf_op jit(solution)/shard_map/ppermute | solution.py:23
  105.1 200.3 %collective-permute-start = (bf16[256,4096]{1,0:T(8,128)(2,1)}, bf16[256,4096]{1,0:T(8,128)(2,1)}, u32[]{:S(2)}, u32[]{:S(2)}) collective-permute-start(bf16[256,4096]{1,0:T(8,128)(2,1)} %param.11), channel_id=1, source_target_pairs={{0,1},{1,2},{2,3},{3,4},{4,5},{5,6},{6,7},{7,8},{8,9},{9,10},{10,1... | collective-permute-start | bytes 6291464 | tf_op jit(solution)/shard_map/ppermute | solution.py:29
  107.8 9.0 %copy-start.10 = (bf16[1,1024,512]{2,1,0:T(8,128)(2,1)}, bf16[1,1024,512]{2,1,0:T(8,128)(2,1)S(1)}, u32[]{:S(2)}) copy-start(bf16[1,1024,512]{2,1,0:T(8,128)(2,1)S(1)} %constant_dynamic-slice_fusion.7) | copy-start | bytes 3145732
  112.8 72.6 %collective-permute-start.7 = (bf16[1024,512]{1,0:T(8,128)(2,1)}, bf16[1024,512]{1,0:T(8,128)(2,1)}, u32[]{:S(2)}, u32[]{:S(2)}) collective-permute-start(bf16[1024,512]{1,0:T(8,128)(2,1)} %get-tuple-element.18), channel_id=1, source_target_pairs={{0,4},{4,0},{8,12},{12,8},{16,20},{20,16},{24,28},{28,24},{1,5},{5... | collective-permute-start | bytes 3145736 | tf_op jit(solution)/shard_map/ppermute | solution.py:23
  116.0 35.1 %collective-permute-start.6 = (bf16[1024,1]{0,1:T(2,128)(2,1)S(1)}, bf16[1024,1]{0,1:T(2,128)(2,1)S(1)}, u32[]{:S(2)}, u32[]{:S(2)}) collective-permute-start(bf16[1024,1]{0,1:T(2,128)(2,1)S(1)} %get-tuple-element.22), channel_id=1, source_target_pairs={{0,4},{4,0},{8,12},{12,8},{16,20},{20,16},{24,28},{28,24},{1,5},{5... | collective-permute-start | bytes 6152 | tf_op jit(solution)/shard_map/ppermute | solution.py:23
  154.1 28.2 %copy-start.9 = (bf16[1024,512]{1,0:T(8,128)(2,1)S(1)}, bf16[1024,512]{1,0:T(8,128)(2,1)}, u32[]{:S(2)}) copy-start(bf16[1024,512]{1,0:T(8,128)(2,1)} %get-tuple-element.19) | copy-start | bytes 3145732
  155.4 28.6 %copy-start.6 = (bf16[2,512,1024]{2,1,0:T(8,128)(2,1)S(1)}, bf16[2,512,1024]{2,1,0:T(8,128)(2,1)}, u32[]{:S(2)}) copy-start(bf16[2,512,1024]{2,1,0:T(8,128)(2,1)} %param.13) | copy-start | bytes 6291460
  155.4 107.0 %collective-permute-start.4 = (bf16[1024,512]{1,0:T(8,128)(2,1)}, bf16[1024,512]{1,0:T(8,128)(2,1)}, u32[]{:S(2)}, u32[]{:S(2)}) collective-permute-start(bf16[1024,512]{1,0:T(8,128)(2,1)} %get-tuple-element.16), channel_id=1, source_target_pairs={{0,4},{4,0},{8,12},{12,8},{16,20},{20,16},{24,28},{28,24},{1,5},{5... | collective-permute-start | bytes 3145736 | tf_op jit(solution)/shard_map/ppermute | solution.py:23
  156.6 200.2 %collective-permute-start.3 = (bf16[256,4096]{0,1:T(8,128)(2,1)}, bf16[256,4096]{0,1:T(8,128)(2,1)}, u32[]{:S(2)}, u32[]{:S(2)}) collective-permute-start(bf16[256,4096]{0,1:T(8,128)(2,1)} %collective-permute-done.2), channel_id=1, source_target_pairs={{0,1},{1,2},{2,3},{3,4},{4,5},{5,6},{6,7},{7,8},{8,9},{9,10},{10,1... | collective-permute-start | bytes 6291464 | tf_op jit(solution)/shard_map/ppermute | solution.py:29
  207.9 5.9 %slice-start.2 = ((s8[4718592]{0:T(1024)(128)(4,1)}), s8[4194304]{0:T(1024)(128)(4,1)S(1)}, s32[]{:S(2)}) async-start(s8[4718592]{0:T(1024)(128)(4,1)} %bitcast.145), calls=%async_computation.7 | async-start | bytes 8388608
  213.8 6.7 %copy-start.14 = (bf16[1024,512]{1,0:T(8,128)(2,1)S(1)}, bf16[1024,512]{1,0:T(8,128)(2,1)}, u32[]{:S(2)}) copy-start(bf16[1024,512]{1,0:T(8,128)(2,1)} %get-tuple-element.17) | copy-start | bytes 3145732
  236.0 13.9 %copy-start.17 = (bf16[512,1024]{1,0:T(8,128)(2,1)}, bf16[512,1024]{1,0:T(8,128)(2,1)S(1)}, u32[]{:S(2)}) copy-start(bf16[512,1024]{1,0:T(8,128)(2,1)S(1)} %add_convert_fusion) | copy-start | bytes 3145732
  302.8 15.1 %collective-permute-start.8 = (bf16[1024,512]{1,0:T(8,128)(2,1)}, bf16[1024,512]{1,0:T(8,128)(2,1)S(1)}, u32[]{:S(2)}, u32[]{:S(2)}) collective-permute-start(bf16[1024,512]{1,0:T(8,128)(2,1)} %get-tuple-element.14), channel_id=1, source_target_pairs={{0,4},{4,0},{8,12},{12,8},{16,20},{20,16},{24,28},{28,24},{1,5},{5... | collective-permute-start | bytes 3145736 | tf_op jit(solution)/shard_map/ppermute | solution.py:23
  305.4 101.9 %collective-permute-start.1 = (bf16[256,4096]{1,0:T(8,128)(2,1)}, bf16[256,4096]{1,0:T(8,128)(2,1)}, u32[]{:S(2)}, u32[]{:S(2)}) collective-permute-start(bf16[256,4096]{1,0:T(8,128)(2,1)} %collective-permute-done), channel_id=1, source_target_pairs={{0,1},{1,2},{2,3},{3,4},{4,5},{5,6},{6,7},{7,8},{8,9},{9,10},{10,1... | collective-permute-start | bytes 6291464 | tf_op jit(solution)/shard_map/ppermute | solution.py:29
  319.9 36.9 %copy-start.2 = (bf16[256,4096]{0,1:T(8,128)(2,1)S(1)}, bf16[256,4096]{0,1:T(8,128)(2,1)}, u32[]{:S(2)}) copy-start(bf16[256,4096]{0,1:T(8,128)(2,1)} %copy.44) | copy-start | bytes 6291460
  319.9 112.0 %all-to-all-start.4 = ((bf16[4,256,1024]{2,1,0:T(8,128)(2,1)}), bf16[4,256,1024]{2,1,0:T(8,128)(2,1)}, u32[]{:S(2)}, u32[]{:S(2)}) async-start(bf16[4,256,1024]{2,1,0:T(8,128)(2,1)} %maximum_select_fusion.1), calls=%async_computation.4 | async-start | bytes 4194304 | tf_op jit(solution)/shard_map/all_to_all | solution.py:199
  441.3 8.9 %copy-start.1 = (bf16[2,1024,512]{2,1,0:T(8,128)(2,1)S(1)}, bf16[2,1024,512]{2,1,0:T(8,128)(2,1)}, u32[]{:S(2)}) copy-start(bf16[2,1024,512]{2,1,0:T(8,128)(2,1)} %param.15) | copy-start | bytes 6291460
  (16 other events, 45.6 us)
where the time goes:
time: 458 us; the launch traced here: 451 us
  matrix products  127 us (28%)
  starting transfers between devices  120 us (26%)
  waiting for transfers between devices  79.6 us (17%)
  other arithmetic  63.1 us (14%)
  local copies, waits for them, and re-layouts  57.2 us (12%)
    ppermute x5, waiting for transfers between devices, swapped(): lax.ppermute(value, axis, [(i, i ^ 1 << apart) for i in range(lax.axis_si...  42.8 us
    all_to_all x1, starting transfers between devices, body(): lax.all_to_all(paired, 'head', split_axis=0, concat_axis=1, tiled=True)  36.9 us
    dot_general x9, matrix products, orthogonal(): jnp.dot(poly_mix, iterate, preferred_element_type=jnp.float32)  35.6 us
    ppermute x4, starting transfers between devices, shifted(): lax.ppermute(value, axis, [(source, source + steps) for source in range(f...  32.4 us
    sub x1, other arithmetic, attend_rows(): weights = jnp.where(allowed, jnp.exp(masked - row_max), 0.0)  30 us
    ppermute x5, starting transfers between devices, swapped(): lax.ppermute(value, axis, [(i, i ^ 1 << apart) for i in range(lax.axis_si...  29.3 us
    dot_general x9, matrix products, orthogonal(): jnp.dot(iterate, iterate.T, preferred_element_type=jnp.float32)  20.1 us
    all_to_all x1, waiting for transfers between devices, body(): lax.all_to_all(values, 'head', split_axis=1, concat_axis=0, tiled=True)  19.8 us
  transfers between devices with their start and end apart: 14, of which 4 were waited for; matrix products, arithmetic and copies ran while one was open for 49% of the time, Pallas kernels for 0%

commit v1 on v0

v1 whole, which is shorter than its diff:
```python
import functools
import math
from types import SimpleNamespace

import jax
import jax.numpy as jnp
from jax import lax
from jax.experimental import pallas as pl
from jax.experimental.pallas import tpu as pltpu
from jax.sharding import PartitionSpec as P

AHD = 128
WINDOW = 512
NS_ITERS = 3
CHUNK = 256

linear_coef = 3.4445
cubic_coef = -4.775
quintic_coef = 2.0315
rms_epsilon = 1e-05
norm_epsilon = 1e-06
MESH = pl.DeviceIdType.MESH
F32 = jnp.float32
BF16 = jnp.bfloat16


def mm(a, b, ca=1, cb=0):
    return lax.dot_general(a, b, (((ca,), (cb,)), ((), ())), preferred_element_type=F32)


def logistic(x):
    return 0.5 * jnp.tanh(0.5 * x) + 0.5


def loop(count, fn):
    def step(i, carry):
        fn(i)
        return carry

    lax.fori_loop(0, count, step, 0)


def at(start, size, multiple):
    return pl.ds(pl.multiple_of(start, multiple), size)


def transpose_down(c):
    def step(i):
        cols = at(i * CHUNK, CHUNK, CHUNK)
        c.wdt[:, cols] = c.wd[cols, :].T

    loop(c.hid_width // CHUNK, step)


def make_targets(c):
    per_block = c.rows // 128

    def step(i):
        rates = c.rates[i // per_block, 0:1, at((i % per_block) * 128, 128, 128)]
        rate_col = jnp.broadcast_to(rates, (128, 128)).T[:, 0:1]
        values = c.v[at(WINDOW + i * 128, 128, 128), :].astype(F32)
        place = i * 128 + lax.broadcasted_iota(jnp.int32, (128, c.width), 0)
        target = jnp.where(place < c.bound, rate_col * values, 0.0)
        c.target[at(i * 128, 128, 128), :] = target.astype(BF16)
        c.target_t[:, at(i * 128, 128, 128)] = target.T.astype(BF16)
        c.k_t[:, at(i * 128, 128, 128)] = c.k[at(WINDOW + i * 128, 128, 128), :].T

    loop(c.high // 128, step)


def backward(c):
    tile = c.tile
    chunks = c.hid_width // CHUNK

    def step(i):
        rows = at((i // chunks) * tile, tile, 128)
        cols = at((i % chunks) * CHUNK, CHUNK, CHUNK)
        k_rows = c.k[at(WINDOW + (i // chunks) * tile, tile, 128), :]
        gate = mm(k_rows, c.wg[:, cols])
        up = mm(k_rows, c.wu[:, cols])
        back = mm(c.target[rows, :], c.wdt[:, cols])
        sig = logistic(gate)
        act = gate * sig
        c.hid[rows, cols] = (act * up).astype(BF16)
        c.d_gate[rows, cols] = (back * up * (sig + act * (1.0 - sig))).astype(BF16)
        c.d_up[rows, cols] = (back * act).astype(BF16)

    loop((c.high // tile) * chunks, step)


def gradients(c):
    def step(i):
        cols = at(i * CHUNK, CHUNK, CHUNK)
        c.grad[0, :, cols] = mm(c.k_t[...], c.d_gate[:, cols])
        c.grad[1, :, cols] = mm(c.k_t[...], c.d_up[:, cols])
        c.grad[2, :, cols] = mm(c.target_t[...], c.hid[:, cols])

    loop(c.hid_width // CHUNK, step)

    def scale(m):
        grad = c.grad[m]
        frob = lax.rsqrt(jnp.sum(grad * grad, keepdims=True) + norm_epsilon)
        c.x[m] = (grad * frob).astype(BF16)

    loop(3, scale)


def newton(c):
    def sweep(_):
        for m in range(3):
            x = c.x[m]
            c.a[m] = mm(x, x, 1, 1).astype(BF16)
        for m in range(3):
            a = c.a[m]
            c.p[m] = (cubic_coef * a.astype(F32) + quintic_coef * mm(a, a)).astype(BF16)
        for m in range(3):
            x = c.x[m]
            c.y[m] = (linear_coef * x.astype(F32) + mm(c.p[m], x)).astype(BF16)
        c.x[...] = c.y[...]

    loop(NS_ITERS, sweep)


def renorm(c):
    def by_column(i):
        cols = at(i * CHUNK, CHUNK, CHUNK)
        for m, ref in ((0, c.wg), (1, c.wu)):
            w = ref[:, cols].astype(F32)
            u = w + c.x[m, :, cols].astype(F32)
            want = jnp.sqrt(jnp.sum(w * w, axis=0, keepdims=True) + norm_epsilon)
            have = jnp.sqrt(jnp.sum(u * u, axis=0, keepdims=True) + norm_epsilon)
            c.x[m, :, cols] = (u * (want / have)).astype(BF16)

    loop(c.hid_width // CHUNK, by_column)

    def by_row(i):
        rows = at(i * 128, 128, 128)
        w = c.wdt[rows, :].astype(F32)
        u = w + c.x[2, rows, :].astype(F32)
        want = jnp.sqrt(jnp.sum(w * w, axis=1, keepdims=True) + norm_epsilon)
        have = jnp.sqrt(jnp.sum(u * u, axis=1, keepdims=True) + norm_epsilon)
        c.x[2, rows, :] = (u * (want / have)).astype(BF16)

    loop(c.width // 128, by_row)


def attention(c):
    tile = WINDOW // 2
    power = math.log2(math.e) / math.sqrt(AHD)

    def step(t):
        rows = at(t * tile, tile, tile)
        span = at(t * tile, WINDOW + tile, tile)
        below = lax.broadcasted_iota(jnp.int32, (tile, tile), 1) <= lax.broadcasted_iota(
            jnp.int32, (tile, tile), 0
        )
        far_bias = jnp.where(c.first_segment * (2 - t) > 0, F32(-1e30), F32(0.0))
        mid_bias = jnp.where(c.first_segment * (1 - t) > 0, F32(-1e30), F32(0.0))
        for head in range(c.width // AHD):
            feats = slice(head * AHD, (head + 1) * AHD)
            scores = mm(c.q[rows, feats], c.k[span, feats], 1, 1)
            edge = jnp.where(below, scores[:, 2 * tile :], scores[:, :tile] + far_bias)
            mid = scores[:, tile : 2 * tile] + mid_bias
            top = jnp.max(jnp.maximum(edge, mid), axis=1, keepdims=True)
            edge = jnp.exp2((edge - top) * power)
            mid = jnp.exp2((mid - top) * power)
            total = jnp.sum(edge + mid, axis=1, keepdims=True)
            weights = jnp.concatenate(
                [
                    jnp.where(below, 0.0, edge).astype(BF16),
                    mid.astype(BF16),
                    jnp.where(below, edge, 0.0).astype(BF16),
                ],
                axis=1,
            )
            mixed = mm(weights, c.v[span, feats])
            c.out[rows, feats] = (mixed / total).astype(BF16)

    loop(c.length // tile, step)


def finish(c, start, raw):
    rows = at(start, raw.shape[0], 128)
    scale = lax.rsqrt(jnp.mean(raw * raw, axis=1, keepdims=True) + rms_epsilon)
    fast = (raw * scale * c.gain).astype(BF16)
    c.out[rows, :] = (c.out[rows, :].astype(F32) + fast.astype(F32)).astype(BF16)


def hidden_rows(c, start, gate_of, up_of):
    q_rows = c.q[at(start, c.tile, 128), :]

    def step(i):
        cols = at(i * CHUNK, CHUNK, CHUNK)
        gate = mm(q_rows, gate_of(cols))
        up = mm(q_rows, up_of(cols))
        c.apply_hid[:, cols] = (gate * logistic(gate) * up).astype(BF16)

    loop(c.hid_width // CHUNK, step)


def apply_old(c, sent=lambda done: None):
    tile = c.tile
    count = c.high // tile

    def body(i):
        hidden_rows(c, i * tile, lambda cols: c.wg[:, cols], lambda cols: c.wu[:, cols])
        c.raw[...] = mm(c.apply_hid[...], c.wd[...])

    def step(i):
        body(i)
        finish(c, i * tile, c.raw[...])

    loop(count - 1, step)
    body(count - 1)
    low_rows = c.low - (count - 1) * tile
    finish(c, (count - 1) * tile, c.raw[:low_rows, :])
    c.mid[...] = c.raw[low_rows:, :]


def apply_new(c, i):
    tile = c.tile
    both = c.high - c.low
    start = c.low + i * tile
    hidden_rows(c, start, lambda cols: c.x[0, :, cols], lambda cols: c.x[1, :, cols])
    raw = mm(c.apply_hid[...], c.x[2], 1, 1)
    if i == 0:
        place = c.low + lax.broadcasted_iota(jnp.int32, (both, c.width), 0)
        finish(c, c.low, jnp.where(place < c.bound, c.mid[...], raw[:both]))
        finish(c, c.low + both, raw[both:])
    else:
        finish(c, start, raw)


def scratch_of(length, width, hid_width):
    low, high = length // 2 - length // 16, length // 2 + length // 16
    tile = high // 3
    return {
        "wg": pltpu.VMEM((width, hid_width), BF16),
        "wu": pltpu.VMEM((width, hid_width), BF16),
        "wd": pltpu.VMEM((hid_width, width), BF16),
        "wdt": pltpu.VMEM((width, hid_width), BF16),
        "target": pltpu.VMEM((high, width), BF16),
        "target_t": pltpu.VMEM((width, high), BF16),
        "k_t": pltpu.VMEM((width, high), BF16),
        "hid": pltpu.VMEM((high, hid_width), BF16),
        "d_gate": pltpu.VMEM((high, hid_width), BF16),
        "d_up": pltpu.VMEM((high, hid_width), BF16),
        "grad": pltpu.VMEM((3, width, hid_width), F32),
        "x": pltpu.VMEM((3, width, hid_width), BF16),
        "y": pltpu.VMEM((3, width, hid_width), BF16),
        "a": pltpu.VMEM((3, width, width), BF16),
        "p": pltpu.VMEM((3, width, width), BF16),
        "apply_hid": pltpu.VMEM((tile, hid_width), BF16),
        "raw": pltpu.VMEM((tile, width), F32),
        "mid": pltpu.VMEM((high - low, width), F32),
        "w_sem": pltpu.SemaphoreType.DMA((3,)),
    }


def sizes(length, width, hid_width, rows):
    low, high = length // 2 - length // 16, length // 2 + length // 16
    return dict(
        length=length, width=width, hid_width=hid_width, rows=rows, low=low, high=high, tile=high // 3
    )


def compute_kernel(
    names, dims, group, bounds, q, k, v, rates, gain, gate_all, up_all, down_all, out, *scratch
):
    c = SimpleNamespace(**dims, **dict(zip(names, scratch)))
    tok, column = lax.axis_index("tok"), lax.axis_index("head")
    parity = tok % 2
    copies = [
        pltpu.make_async_copy(whole.at[parity], mine, c.w_sem.at[i])
        for i, (whole, mine) in enumerate(((gate_all, c.wg), (up_all, c.wu), (down_all, c.wd)))
    ]
    for copy in copies:
        copy.start()
    c.q, c.k, c.v, c.rates, c.out = q, k, v, rates, out
    c.gain = gain[2 * column + parity]
    c.bound = bounds[tok // 2]
    c.first_segment = jnp.where(tok < 2, 1, 0)
    for copy in copies:
        copy.wait()
    transpose_down(c)
    make_targets(c)
    backward(c)
    gradients(c)
    newton(c)
    renorm(c)
    attention(c)
    apply_old(c)
    for i in range(3):
        apply_new(c, i)


def flip(index, distance, count):
    result, place = 0, 1
    while place < count:
        bit = (index // place) % 2
        result = result + place * (1 - bit if distance & place else bit)
        place *= 2
    return result


def distances(peers):
    return sorted(range(1, peers), key=lambda d: (d < 2, d % 2, d))


def place_of(peer, tok, group):
    return (tok - tok % 2 + peer // group, peer % group)


def feature_of(peer, group):
    return 2 * (peer % group) + peer // group


def greet(others):
    barrier = pltpu.get_barrier_semaphore()
    for other in others:
        pl.semaphore_signal(barrier, inc=1, device_id=other, device_id_type=MESH)
    pl.semaphore_wait(barrier, len(others))


def gather_kernel(
    group, toks, width, q, k, v, r, oq, ok, ov, orate, send, recv, own_sem, halo_send, halo_recv
):
    tok, column = lax.axis_index("tok"), lax.axis_index("head")
    peers = 2 * group
    me = (tok % 2) * group + column
    after = ((tok + 2) % toks, column)
    before = ((tok + toks - 2) % toks, column)
    rows = q.shape[0]
    reach = WINDOW // rows
    greet([place_of(flip(me, d, peers), tok, group) for d in range(1, peers)] + [after, before])

    def source(t, peer):
        j = feature_of(peer, group)
        if t == 3:
            return r.at[j]
        return (k, v, q)[t].at[:, at(j * width, width, width)]

    def slot(t, peer):
        return (ok.at[reach + peer], ov.at[reach + peer], oq.at[peer], orate.at[peer])[t]

    def remote(t, d):
        peer = flip(me, d, peers)
        return pltpu.make_async_remote_copy(
            source(t, peer), slot(t, me), send.at[t, d], recv.at[t, d],
            device_id=place_of(peer, tok, group), device_id_type=MESH,
        )

    def arrival(t, d):
        peer = flip(me, d, peers)
        return pltpu.make_async_remote_copy(
            slot(t, peer), slot(t, peer), send.at[t, d], recv.at[t, d],
            device_id=place_of(peer, tok, group), device_id_type=MESH,
        )

    own = [pltpu.make_async_copy(source(t, me), slot(t, me), own_sem.at[t]) for t in range(4)]
    for t in (3, 0, 1, 2):
        for d in distances(peers):
            remote(t, d).start()
        own[t].start()
    for t in (3, 0, 1):
        for d in distances(peers):
            arrival(t, d).wait_recv()
        own[t].wait()
    halos = [
        pltpu.make_async_remote_copy(
            o.at[pl.ds(peers, reach)], o.at[pl.ds(0, reach)], halo_send.at[t], halo_recv.at[t],
            device_id=after, device_id_type=MESH,
        )
        for t, o in enumerate((ok, ov))
    ]
    for halo in halos:
        halo.start()
    for d in distances(peers):
        arrival(2, d).wait_recv()
    own[2].wait()
    for halo in halos:
        halo.wait()
    for t in range(4):
        for d in distances(peers):
            remote(t, d).wait_send()


def scatter_kernel(group, item, out, send, recv, own_sem):
    tok, column = lax.axis_index("tok"), lax.axis_index("head")
    peers = 2 * group
    me = (tok % 2) * group + column
    width = item.shape[2]
    greet([place_of(flip(me, d, peers), tok, group) for d in range(1, peers)])

    def block(peer):
        return out.at[:, at(feature_of(peer, group) * width, width, width)]

    def remote(d):
        peer = flip(me, d, peers)
        return pltpu.make_async_remote_copy(
            item.at[peer], block(me), send.at[d], recv.at[d],
            device_id=place_of(peer, tok, group), device_id_type=MESH,
        )

    def arrival(d):
        peer = flip(me, d, peers)
        return pltpu.make_async_remote_copy(
            item.at[peer], block(peer), send.at[d], recv.at[d],
            device_id=place_of(peer, tok, group), device_id_type=MESH,
        )

    own = pltpu.make_async_copy(item.at[me], block(me), own_sem)
    own.start()
    for d in distances(peers):
        remote(d).start()
    own.wait()
    for d in distances(peers):
        arrival(d).wait_recv()
    for d in distances(peers):
        remote(d).wait_send()


def body(queries, keys, values, token_rates, gate_start, up_start, down_start, norm_gain, bounds):
    rows, feats = queries.shape
    group, toks = lax.axis_size("head"), lax.axis_size("tok")
    heads, width, hid_width = token_rates.shape[1], gate_start.shape[1], gate_start.shape[2]
    peers = 2 * group
    length = peers * rows
    reach = WINDOW // rows
    anywhere = pl.BlockSpec(memory_space=pl.ANY)
    vmem = pl.BlockSpec(memory_space=pltpu.VMEM)
    dma = pltpu.SemaphoreType.DMA
    rates = jnp.broadcast_to(token_rates.T.astype(F32)[:, None, :], (heads, 8, rows))
    blocks = jax.ShapeDtypeStruct((peers, rows, width), BF16)
    wide = jax.ShapeDtypeStruct((reach + peers, rows, width), BF16)
    item_q, item_k, item_v, item_r = pl.pallas_call(
        functools.partial(gather_kernel, group, toks, width),
        out_shape=(blocks, wide, wide, jax.ShapeDtypeStruct((peers, 8, rows), F32)),
        in_specs=[anywhere] * 4,
        out_specs=[anywhere] * 4,
        scratch_shapes=[dma((4, peers)), dma((4, peers)), dma((4,)), dma((2,)), dma((2,))],
        compiler_params=pltpu.CompilerParams(collective_id=0, has_side_effects=True),
        name="gather",
    )(queries, keys, values, rates)
    scratch = scratch_of(length, width, hid_width)
    item = pl.pallas_call(
        functools.partial(
            compute_kernel, tuple(scratch), sizes(length, width, hid_width, rows), group
        ),
        out_shape=jax.ShapeDtypeStruct((length, width), BF16),
        in_specs=[pl.BlockSpec(memory_space=pltpu.SMEM)] + [vmem] * 5 + [anywhere] * 3,
        out_specs=vmem,
        scratch_shapes=list(scratch.values()),
        compiler_params=pltpu.CompilerParams(vmem_limit_bytes=64000000),
        name="compute",
    )(
        bounds,
        item_q.reshape(length, width),
        item_k.reshape(-1, width),
        item_v.reshape(-1, width),
        item_r,
        norm_gain.reshape(heads, 1, width),
        gate_start,
        up_start,
        down_start,
    )
    return pl.pallas_call(
        functools.partial(scatter_kernel, group),
        out_shape=jax.ShapeDtypeStruct((rows, feats), BF16),
        in_specs=[anywhere],
        out_specs=anywhere,
        scratch_shapes=[dma((peers,)), dma((peers,)), dma],
        compiler_params=pltpu.CompilerParams(collective_id=1, has_side_effects=True),
        name="scatter",
    )(item.reshape(peers, rows, width))


def solution(mesh):
    spread = P(("tok", "head"), None)
    owned = P("head", None, None)
    return jax.shard_map(
        body,
        mesh=mesh,
        in_specs=(spread,) * 4 + (owned,) * 3 + (P(), P()),
        out_specs=spread,
        check_vma=False,
    )
```

time: 458 us -> 176 us (0.38)
  the two profiles are of different devices: /device:TPU:11 before, /device:TPU:0 now
where the time goes in v1:
time: 176 us
  Pallas kernels  171 us (97%)
  local copies, waits for them, and re-layouts  3.77 us (2%)
    pallas_call x1, Pallas kernels, body(): pl.pallas_call(functools.partial(gather_kernel, group, toks, width), out_...  79.4 us
    pallas_call x1, Pallas kernels, body(): pl.pallas_call(functools.partial(compute_kernel, tuple(scratch), sizes(le...  65.5 us
    pallas_call x1, Pallas kernels, body(): pl.pallas_call(functools.partial(scatter_kernel, group), out_shape=jax.Sh...  26.4 us

profile of v1, /device:TPU:0, one launch (start us, length us, event | category | flops | bytes accessed | tf_op | source)
XLA Modules:
  0.0 175.9 jit_solution(6844473629987605137)
XLA Ops:
  0.0 0.7 convert_bitcast_fusion
  0.7 0.6 broadcast_in_dim.2.r
  1.3 79.4 %gather.1 = (bf16[8,256,512]{2,1,0:T(8,128)(2,1)}, bf16[10,256,512]{2,1,0:T(8,128)(2,1)}, bf16[10,256,512]{2,1,0:T(8,128)(2,1)}, f32[8,8,256]{2,1,0:T(8,128)}) custom-call(bf16[256,4096]{1,0:T(8,128)(2,1)} %q.1, bf16[256,4096]{1,0:T(8,128)(2,1)} %k.1, bf16[256,4096]{1,0:T(8,128)(2,1)} %v.1, f32[8,8,256]{2,1,0:T(8,128)} %broadcast_in_dim.2.r), custom_call_target="tpu_custom_call" | custom-call | tf_op jit(solution)/shard_map/gather/pallas_call | solution.py:436
  80.8 65.5 %compute.1 = bf16[2048,512]{1,0:T(8,128)(2,1)} custom-call(s32[4]{0:T(128)} %bounds.1, bf16[2048,512]{1,0:T(8,128)(2,1)} %bitcast.10, bf16[2560,512]{1,0:T(8,128)(2,1)} %bitcast.8, bf16[2560,512]{1,0:T(8,128)(2,1)} %bitcast.9, f32[8,8,256]{2,1,0:T(8,128)} %get-tuple-element.12.rates, f32[8,1,512]{2,1,0:T(1,128)} %bitcast.11, bf16[2,512,1024]{2,1,0:T(8,128)(2,1)} %gate_all.1, ...), custom_call_target="tpu_custom_call" | custom-call | tf_op jit(solution)/shard_map/compute/pallas_call | solution.py:446
  146.3 26.4 %scatter.1 = bf16[256,4096]{1,0:T(8,128)(2,1)} custom-call(bf16[8,256,512]{2,1,0:T(8,128)(2,1)} %bitcast.7), custom_call_target="tpu_custom_call" | custom-call | tf_op jit(solution)/shard_map/scatter/pallas_call | solution.py:467
  172.7 3.1 %copy.11 = bf16[256,4096]{1,0:T(8,128)(2,1)} copy(bf16[256,4096]{1,0:T(8,128)(2,1)} %scatter.1) | data formatting | bytes 4194304

commit v2 on v1

v2 whole, which is shorter than its diff:
```python
import functools
import math
from types import SimpleNamespace

import jax
import jax.numpy as jnp
from jax import lax
from jax.experimental import pallas as pl
from jax.experimental.pallas import tpu as pltpu
from jax.sharding import PartitionSpec as P

AHD = 128
WINDOW = 512
NS_ITERS = 3
CHUNK = 256

linear_coef = 3.4445
cubic_coef = -4.775
quintic_coef = 2.0315
rms_epsilon = 1e-05
norm_epsilon = 1e-06
MESH = pl.DeviceIdType.MESH
F32 = jnp.float32
BF16 = jnp.bfloat16


def mm(a, b, ca=1, cb=0):
    return lax.dot_general(a, b, (((ca,), (cb,)), ((), ())), preferred_element_type=F32)


def logistic(x):
    return 0.5 * jnp.tanh(0.5 * x) + 0.5


def loop(count, fn):
    def step(i, carry):
        fn(i)
        return carry

    lax.fori_loop(0, count, step, 0)


def at(start, size, multiple):
    return pl.ds(pl.multiple_of(start, multiple), size)


def transpose_down(c):
    def step(i):
        cols = at(i * CHUNK, CHUNK, CHUNK)
        c.wdt[:, cols] = c.wd[cols, :].T

    loop(c.hid_width // CHUNK, step)


def transpose_keys(c):
    def step(i):
        c.k_t[:, at(i * 128, 128, 128)] = c.k[at(WINDOW + i * 128, 128, 128), :].T

    loop(c.high // 128, step)


def make_targets(c):
    per_block = c.rows // 128

    def step(i):
        rates = c.rates[i // per_block, 0:1, at((i % per_block) * 128, 128, 128)]
        rate_col = jnp.broadcast_to(rates, (128, 128)).T[:, 0:1]
        values = c.v[at(WINDOW + i * 128, 128, 128), :].astype(F32)
        place = i * 128 + lax.broadcasted_iota(jnp.int32, (128, c.width), 0)
        target = jnp.where(place < c.bound, rate_col * values, 0.0)
        c.target[at(i * 128, 128, 128), :] = target.astype(BF16)
        c.target_t[:, at(i * 128, 128, 128)] = target.T.astype(BF16)

    loop(c.high // 128, step)


def forward(c):
    chunks = c.hid_width // CHUNK

    def step(i):
        rows = at((i // chunks) * c.tile, c.tile, 128)
        cols = at((i % chunks) * CHUNK, CHUNK, CHUNK)
        k_rows = c.k[at(WINDOW + (i // chunks) * c.tile, c.tile, 128), :]
        gate = mm(k_rows, c.wg[:, cols])
        up = mm(k_rows, c.wu[:, cols])
        sig = logistic(gate)
        act = gate * sig
        c.hid[rows, cols] = (act * up).astype(BF16)
        c.act[rows, cols] = act
        c.slope[rows, cols] = up * (sig + act * (1.0 - sig))

    loop((c.high // c.tile) * chunks, step)


def backward(c):
    chunks = c.hid_width // CHUNK

    def step(i):
        rows = at((i // chunks) * c.tile, c.tile, 128)
        cols = at((i % chunks) * CHUNK, CHUNK, CHUNK)
        back = mm(c.target[rows, :], c.wdt[:, cols])
        c.d_gate[rows, cols] = (back * c.slope[rows, cols]).astype(BF16)
        c.d_up[rows, cols] = (back * c.act[rows, cols]).astype(BF16)

    loop((c.high // c.tile) * chunks, step)


def gradients(c):
    def step(i):
        cols = at(i * CHUNK, CHUNK, CHUNK)
        c.grad[0, :, cols] = mm(c.k_t[...], c.d_gate[:, cols])
        c.grad[1, :, cols] = mm(c.k_t[...], c.d_up[:, cols])
        c.grad[2, :, cols] = mm(c.target_t[...], c.hid[:, cols])

    loop(c.hid_width // CHUNK, step)

    def scale(m):
        grad = c.grad[m]
        frob = lax.rsqrt(jnp.sum(grad * grad, keepdims=True) + norm_epsilon)
        c.x[0, m] = (grad * frob).astype(BF16)

    loop(3, scale)


def newton(c):
    def sweep(turn):
        old, new = turn % 2, (turn + 1) % 2
        for m in range(3):
            x = c.x[old, m]
            c.a[m] = mm(x, x, 1, 1).astype(BF16)
        for m in range(3):
            a = c.a[m]
            c.p[m] = (cubic_coef * a.astype(F32) + quintic_coef * mm(a, a)).astype(BF16)
        for m in range(3):
            x = c.x[old, m]
            c.x[new, m] = (linear_coef * x.astype(F32) + mm(c.p[m], x)).astype(BF16)

    loop(NS_ITERS, sweep)


def renorm(c):
    def by_column(i):
        cols = at(i * CHUNK, CHUNK, CHUNK)
        for m, ref in ((0, c.wg), (1, c.wu)):
            w = ref[:, cols].astype(F32)
            u = w + c.x[NS_ITERS % 2, m, :, cols].astype(F32)
            want = jnp.sqrt(jnp.sum(w * w, axis=0, keepdims=True) + norm_epsilon)
            have = jnp.sqrt(jnp.sum(u * u, axis=0, keepdims=True) + norm_epsilon)
            c.x[NS_ITERS % 2, m, :, cols] = (u * (want / have)).astype(BF16)

    loop(c.hid_width // CHUNK, by_column)

    def by_row(i):
        rows = at(i * 128, 128, 128)
        w = c.wdt[rows, :].astype(F32)
        u = w + c.x[NS_ITERS % 2, 2, rows, :].astype(F32)
        want = jnp.sqrt(jnp.sum(w * w, axis=1, keepdims=True) + norm_epsilon)
        have = jnp.sqrt(jnp.sum(u * u, axis=1, keepdims=True) + norm_epsilon)
        c.x[NS_ITERS % 2, 2, rows, :] = (u * (want / have)).astype(BF16)

    loop(c.width // 128, by_row)


def attention(c, first, count):
    tile = WINDOW // 2
    power = math.log2(math.e) / math.sqrt(AHD)

    def step(i):
        t = first + i
        rows = at(t * tile, tile, tile)
        span = at(t * tile, WINDOW + tile, tile)
        below = lax.broadcasted_iota(jnp.int32, (tile, tile), 1) <= lax.broadcasted_iota(
            jnp.int32, (tile, tile), 0
        )
        far_bias = jnp.where(c.first_segment * (2 - t) > 0, F32(-1e30), F32(0.0))
        mid_bias = jnp.where(c.first_segment * (1 - t) > 0, F32(-1e30), F32(0.0))
        for head in range(c.width // AHD):
            feats = slice(head * AHD, (head + 1) * AHD)
            scores = mm(c.q[rows, feats], c.k[span, feats], 1, 1)
            edge = jnp.where(below, scores[:, 2 * tile :], scores[:, :tile] + far_bias)
            mid = scores[:, tile : 2 * tile] + mid_bias
            top = jnp.max(jnp.maximum(edge, mid), axis=1, keepdims=True)
            edge = jnp.exp2((edge - top) * power)
            mid = jnp.exp2((mid - top) * power)
            total = jnp.sum(edge + mid, axis=1, keepdims=True)
            weights = jnp.concatenate(
                [
                    jnp.where(below, 0.0, edge).astype(BF16),
                    mid.astype(BF16),
                    jnp.where(below, edge, 0.0).astype(BF16),
                ],
                axis=1,
            )
            mixed = mm(weights, c.v[span, feats])
            c.out[rows, feats] = (mixed / total).astype(BF16)

    loop(count, step)


def swiglu(c, start, gate, up, down, down_dim):
    q_rows = c.q[at(start, c.rows, c.rows), :]

    def step(i):
        cols = at(i * CHUNK, CHUNK, CHUNK)
        pre_gate = mm(q_rows, gate[:, cols])
        pre_up = mm(q_rows, up[:, cols])
        c.apply_hid[:, cols] = (pre_gate * logistic(pre_gate) * pre_up).astype(BF16)

    loop(c.hid_width // CHUNK, step)
    return mm(c.apply_hid[...], down[...], 1, down_dim)


def fast_rows(c, start):
    new = c.x.at[NS_ITERS % 2]

    @pl.when(start < c.high)
    def _():
        c.raw[...] = swiglu(c, start, c.wg, c.wu, c.wd, 0)

    @pl.when(start + c.rows > c.low)
    def _():
        after = swiglu(c, start, new.at[0], new.at[1], new.at[2], 1)
        place = start + lax.broadcasted_iota(jnp.int32, after.shape, 0)
        kept = (place < c.bound) & (place < c.high)
        c.raw[...] = jnp.where(kept, c.raw[...], after)

    raw = c.raw[...]
    rows = at(start, c.rows, c.rows)
    scale = lax.rsqrt(jnp.mean(raw * raw, axis=1, keepdims=True) + rms_epsilon)
    fast = (raw * scale * c.gain).astype(BF16)
    c.out[rows, :] = (c.out[rows, :].astype(F32) + fast.astype(F32)).astype(BF16)


def scratch_of(length, width, hid_width, rows, peers):
    low, high = length // 2 - length // 16, length // 2 + length // 16
    dma = pltpu.SemaphoreType.DMA
    return {
        "q": pltpu.VMEM((length, width), BF16),
        "k": pltpu.VMEM((WINDOW + length, width), BF16),
        "v": pltpu.VMEM((WINDOW + length, width), BF16),
        "rates": pltpu.VMEM((peers, 8, rows), F32),
        "out": pltpu.VMEM((length, width), BF16),
        "send": dma((4, peers)),
        "recv": dma((4, peers)),
        "own_sem": dma((4,)),
        "halo_send": dma((2,)),
        "halo_recv": dma((2,)),
        "out_send": dma((peers,)),
        "out_recv": dma((peers,)),
        "out_own": dma,
        "wg": pltpu.VMEM((width, hid_width), BF16),
        "wu": pltpu.VMEM((width, hid_width), BF16),
        "wd": pltpu.VMEM((hid_width, width), BF16),
        "wdt": pltpu.VMEM((width, hid_width), BF16),
        "target": pltpu.VMEM((high, width), BF16),
        "target_t": pltpu.VMEM((width, high), BF16),
        "k_t": pltpu.VMEM((width, high), BF16),
        "hid": pltpu.VMEM((high, hid_width), BF16),
        "d_gate": pltpu.VMEM((high, hid_width), BF16),
        "d_up": pltpu.VMEM((high, hid_width), BF16),
        "grad": pltpu.VMEM((3, width, hid_width), F32),
        "x": pltpu.VMEM((2, 3, width, hid_width), BF16),
        "act": pltpu.VMEM((high, hid_width), F32),
        "slope": pltpu.VMEM((high, hid_width), F32),
        "a": pltpu.VMEM((3, width, width), BF16),
        "p": pltpu.VMEM((3, width, width), BF16),
        "apply_hid": pltpu.VMEM((rows, hid_width), BF16),
        "raw": pltpu.VMEM((rows, width), F32),
        "w_sem": dma((3,)),
    }


def sizes(length, width, hid_width, rows):
    low, high = length // 2 - length // 16, length // 2 + length // 16
    return dict(
        length=length, width=width, hid_width=hid_width, rows=rows, low=low, high=high, tile=high // 3
    )


def flip(index, distance, count):
    result, place = 0, 1
    while place < count:
        bit = (index // place) % 2
        result = result + place * (1 - bit if distance & place else bit)
        place *= 2
    return result


def distances(peers):
    return sorted(range(1, peers), key=lambda d: (d < 2, d % 2, d))


def order_of(step, peers):
    half = peers // 2
    return jnp.where(
        step < half - 1, 2 * step + 2, jnp.where(step < peers - 2, 2 * (step - half) + 5, peers - 1 - step)
    )


def flip_by(index, distance, count):
    result, place = 0, 1
    while place < count:
        bit, other = (index // place) % 2, (distance // place) % 2
        result = result + place * (bit + other - 2 * bit * other)
        place *= 2
    return result


def place_of(peer, tok, group):
    return (tok - tok % 2 + peer // group, peer % group)


def feature_of(peer, group):
    return 2 * (peer % group) + peer // group


def greet(others):
    barrier = pltpu.get_barrier_semaphore()
    for other in others:
        pl.semaphore_signal(barrier, inc=1, device_id=other, device_id_type=MESH)
    pl.semaphore_wait(barrier, len(others))


def kernel(
    names, dims, group, toks, bounds, gain, q, k, v, r, gate_all, up_all, down_all, out, *scratch
):
    c = SimpleNamespace(**dims, **dict(zip(names, scratch)))
    tok, column = lax.axis_index("tok"), lax.axis_index("head")
    parity = tok % 2
    peers, rows, width = 2 * group, c.rows, c.width
    me = parity * group + column
    after = ((tok + 2) % toks, column)
    before = ((tok + toks - 2) % toks, column)
    weights = [
        pltpu.make_async_copy(whole.at[parity], mine, c.w_sem.at[i])
        for i, (whole, mine) in enumerate(((gate_all, c.wg), (up_all, c.wu), (down_all, c.wd)))
    ]
    for copy in weights:
        copy.start()
    c.gain = gain[2 * column + parity]
    c.bound = bounds[tok // 2]
    c.first_segment = jnp.where(tok < 2, 1, 0)
    greet([place_of(flip(me, d, peers), tok, group) for d in range(1, peers)] + [after, before])

    def source(t, peer):
        j = feature_of(peer, group)
        if t == 3:
            return r.at[j]
        return (k, v, q)[t].at[:, at(j * width, width, width)]

    def slot(t, peer):
        if t == 3:
            return c.rates.at[peer]
        shift = WINDOW if t < 2 else 0
        return (c.k, c.v, c.q)[t].at[at(shift + peer * rows, rows, rows), :]

    def remote(t, peer):
        return pltpu.make_async_remote_copy(
            source(t, peer), slot(t, me), c.send.at[t, peer], c.recv.at[t, me],
            device_id=place_of(peer, tok, group), device_id_type=MESH,
        )

    def own(t):
        return pltpu.make_async_copy(source(t, me), slot(t, me), c.own_sem.at[t])

    def arrived(t, peer):
        @pl.when(me != peer)
        def _():
            pltpu.make_async_remote_copy(
                slot(t, peer), slot(t, peer), c.send.at[t, peer], c.recv.at[t, peer],
                device_id=place_of(peer, tok, group), device_id_type=MESH,
            ).wait_recv()

        @pl.when(me == peer)
        def _():
            own(t).wait()

    def block(peer):
        return out.at[:, at(feature_of(peer, group) * width, width, width)]

    def done_rows(peer):
        return c.out.at[at(peer * rows, rows, rows), :]

    def give(peer):
        return pltpu.make_async_remote_copy(
            done_rows(peer), block(me), c.out_send.at[peer], c.out_recv.at[me],
            device_id=place_of(peer, tok, group), device_id_type=MESH,
        )

    def taken(peer):
        return pltpu.make_async_remote_copy(
            done_rows(peer), block(peer), c.out_send.at[peer], c.out_recv.at[peer],
            device_id=place_of(peer, tok, group), device_id_type=MESH,
        )

    order = distances(peers)
    for t in (3, 0, 1, 2):
        for d in order:
            remote(t, flip(me, d, peers)).start()
        own(t).start()
    for copy in weights:
        copy.wait()
    transpose_down(c)
    needed = -(-c.high // rows)
    for p in range(needed):
        arrived(0, p)
    forward(c)
    transpose_keys(c)
    for p in range(peers):
        arrived(3, p)
    for p in range(needed):
        arrived(1, p)
    make_targets(c)
    backward(c)
    gradients(c)
    for t in (0, 1):
        for p in range(needed, peers):
            arrived(t, p)
    halos = [
        pltpu.make_async_remote_copy(
            o.at[pl.ds(c.length, WINDOW), :], o.at[pl.ds(0, WINDOW), :],
            c.halo_send.at[t], c.halo_recv.at[t], device_id=after, device_id_type=MESH,
        )
        for t, o in enumerate((c.k, c.v))
    ]
    for halo in halos:
        halo.start()
    newton(c)
    renorm(c)
    for p in range(peers):
        arrived(2, p)
    for halo in halos:
        halo.wait()
    tiles = rows // (WINDOW // 2)

    def turn(step):
        peer = flip_by(me, order_of(step, peers), peers)
        attention(c, peer * tiles, tiles)
        fast_rows(c, peer * rows)

        @pl.when(peer != me)
        def _():
            give(peer).start()

        @pl.when(peer == me)
        def _():
            pltpu.make_async_copy(done_rows(me), block(me), c.out_own).start()

    loop(peers, turn)
    pltpu.make_async_copy(done_rows(me), block(me), c.out_own).wait()
    for d in order:
        taken(flip(me, d, peers)).wait_recv()
    for d in order:
        give(flip(me, d, peers)).wait_send()
        for t in range(4):
            remote(t, flip(me, d, peers)).wait_send()


def body(queries, keys, values, token_rates, gate_start, up_start, down_start, norm_gain, bounds):
    rows, feats = queries.shape
    group, toks = lax.axis_size("head"), lax.axis_size("tok")
    heads, width, hid_width = token_rates.shape[1], gate_start.shape[1], gate_start.shape[2]
    peers = 2 * group
    length = peers * rows
    anywhere = pl.BlockSpec(memory_space=pl.ANY)
    vmem = pl.BlockSpec(memory_space=pltpu.VMEM)
    dma = pltpu.SemaphoreType.DMA
    rates = jnp.broadcast_to(token_rates.T.astype(F32)[:, None, :], (heads, 8, rows))
    scratch = scratch_of(length, width, hid_width, rows, peers)
    return pl.pallas_call(
        functools.partial(
            kernel, tuple(scratch), sizes(length, width, hid_width, rows), group, toks
        ),
        out_shape=jax.ShapeDtypeStruct((rows, feats), BF16),
        in_specs=[pl.BlockSpec(memory_space=pltpu.SMEM), vmem] + [anywhere] * 7,
        out_specs=anywhere,
        scratch_shapes=list(scratch.values()),
        compiler_params=pltpu.CompilerParams(
            collective_id=0, has_side_effects=True, vmem_limit_bytes=66000000
        ),
        name="layer",
    )(
        bounds, norm_gain.reshape(heads, 1, width), queries, keys, values, rates,
        gate_start, up_start, down_start,
    )


def solution(mesh):
    spread = P(("tok", "head"), None)
    owned = P("head", None, None)
    return jax.shard_map(
        body,
        mesh=mesh,
        in_specs=(spread,) * 4 + (owned,) * 3 + (P(), P()),
        out_specs=spread,
        check_vma=False,
    )
```

time: 176 us -> 132 us (0.75)
  Pallas kernels: 171 us -> 127 us
    pallas_call x3 -> x1, Pallas kernels: 171 us -> 127 us  [body(): pl.pallas_call(functools.partial(kernel, tuple(scratch), sizes(length, wi...]
where the time goes in v2:
time: 132 us
  Pallas kernels  127 us (96%)
  local copies, waits for them, and re-layouts  3.77 us (3%)
    pallas_call x1, Pallas kernels, body(): pl.pallas_call(functools.partial(kernel, tuple(scratch), sizes(length, wi...  127 us
    unnamed x1, local copies, waits for them, and re-layouts  3.13 us

profile of v2, /device:TPU:0, one launch (start us, length us, event | category | flops | bytes accessed | tf_op | source)
XLA Modules:
  0.0 131.6 jit_solution(9384021318077711547)
XLA Ops:
  0.0 0.7 convert_bitcast_fusion
  0.7 0.6 broadcast_in_dim.2.r
  1.3 127.1 %layer.1 = bf16[256,4096]{1,0:T(8,128)(2,1)} custom-call(s32[4]{0:T(128)} %bounds.1, f32[8,1,512]{2,1,0:T(1,128)} %bitcast.3, bf16[256,4096]{1,0:T(8,128)(2,1)} %q.1, bf16[256,4096]{1,0:T(8,128)(2,1)} %k.1, bf16[256,4096]{1,0:T(8,128)(2,1)} %v.1, f32[8,8,256]{2,1,0:T(8,128)} %broadcast_in_dim.2.r, bf16[2,512,1024]{2,1,0:T(8,128)(2,1)} %gate_all.1, ...), custom_call_target="tpu_custom_call" | custom-call | tf_op jit(solution)/shard_map/layer/pallas_call | solution.py:470
  128.5 3.1 %copy.11 = bf16[256,4096]{1,0:T(8,128)(2,1)} copy(bf16[256,4096]{1,0:T(8,128)(2,1)} %layer.1) | data formatting | bytes 4194304

commit v3 on v2

--- a/solution.py
+++ b/solution.py
@@ -12,7 +12,7 @@
 AHD = 128
 WINDOW = 512
 NS_ITERS = 3
-CHUNK = 256
+CHUNK = 512
 
 linear_coef = 3.4445
 cubic_coef = -4.775
@@ -287,7 +287,7 @@
 
 
 def distances(peers):
-    return sorted(range(1, peers), key=lambda d: (d < 2, d % 2, d))
+    return sorted(range(1, peers), key=lambda d: (d > 1, d % 2, d))
 
 
 def order_of(step, peers):
@@ -394,18 +394,27 @@
         )
 
     order = distances(peers)
-    for t in (3, 0, 1, 2):
+    for t in (3, 0):
         for d in order:
             remote(t, flip(me, d, peers)).start()
         own(t).start()
+
+    def send_next(t):
+        for d in order:
+            remote(t - 1, flip(me, d, peers)).wait_send()
+            remote(t, flip(me, d, peers)).start()
+        own(t).start()
+
     for copy in weights:
         copy.wait()
     transpose_down(c)
+    send_next(1)
     needed = -(-c.high // rows)
     for p in range(needed):
         arrived(0, p)
     forward(c)
     transpose_keys(c)
+    send_next(2)
     for p in range(peers):
         arrived(3, p)
     for p in range(needed):
@@ -452,7 +461,7 @@
         taken(flip(me, d, peers)).wait_recv()
     for d in order:
         give(flip(me, d, peers)).wait_send()
-        for t in range(4):
+        for t in (2, 3):
             remote(t, flip(me, d, peers)).wait_send()
 
 

time: 132 us -> 128 us (0.970)
  Pallas kernels: 127 us -> 123 us
    pallas_call x1, Pallas kernels: 127 us -> 123 us  [body(): pl.pallas_call(functools.partial(kernel, tuple(scratch), sizes(length, wi...]
where the time goes in v3:
time: 128 us; the launch traced here: 127 us
  Pallas kernels  123 us (96%)
  local copies, waits for them, and re-layouts  3.77 us (3%)
    pallas_call x1, Pallas kernels, body(): pl.pallas_call(functools.partial(kernel, tuple(scratch), sizes(length, wi...  123 us
    unnamed x1, local copies, waits for them, and re-layouts  3.13 us

profile of v3, /device:TPU:0, one launch (start us, length us, event | category | flops | bytes accessed | tf_op | source)
XLA Modules:
  0.0 127.2 jit_solution(658251984892944527)
XLA Ops:
  0.0 0.7 convert_bitcast_fusion
  0.7 0.6 broadcast_in_dim.2.r
  1.3 122.7 %layer.1 = bf16[256,4096]{1,0:T(8,128)(2,1)} custom-call(s32[4]{0:T(128)} %bounds.1, f32[8,1,512]{2,1,0:T(1,128)} %bitcast.3, bf16[256,4096]{1,0:T(8,128)(2,1)} %q.1, bf16[256,4096]{1,0:T(8,128)(2,1)} %k.1, bf16[256,4096]{1,0:T(8,128)(2,1)} %v.1, f32[8,8,256]{2,1,0:T(8,128)} %broadcast_in_dim.2.r, bf16[2,512,1024]{2,1,0:T(8,128)(2,1)} %gate_all.1, ...), custom_call_target="tpu_custom_call" | custom-call | tf_op jit(solution)/shard_map/layer/pallas_call | solution.py:479
  124.1 3.1 %copy.11 = bf16[256,4096]{1,0:T(8,128)(2,1)} copy(bf16[256,4096]{1,0:T(8,128)(2,1)} %layer.1) | data formatting | bytes 4194304

commit v4 on v3

--- a/solution.py
+++ b/solution.py
@@ -399,6 +399,14 @@
             remote(t, flip(me, d, peers)).start()
         own(t).start()
 
+    halos = [
+        pltpu.make_async_remote_copy(
+            o.at[pl.ds(c.length, WINDOW), :], o.at[pl.ds(0, WINDOW), :],
+            c.halo_send.at[t], c.halo_recv.at[t], device_id=after, device_id_type=MESH,
+        )
+        for t, o in enumerate((c.k, c.v))
+    ]
+
     def send_next(t):
         for d in order:
             remote(t - 1, flip(me, d, peers)).wait_send()
@@ -412,6 +420,9 @@
     needed = -(-c.high // rows)
     for p in range(needed):
         arrived(0, p)
+    for p in range(needed, peers):
+        arrived(0, p)
+    halos[0].start()
     forward(c)
     transpose_keys(c)
     send_next(2)
@@ -419,31 +430,21 @@
         arrived(3, p)
     for p in range(needed):
         arrived(1, p)
+    for p in range(needed, peers):
+        arrived(1, p)
+    halos[1].start()
     make_targets(c)
     backward(c)
     gradients(c)
-    for t in (0, 1):
-        for p in range(needed, peers):
-            arrived(t, p)
-    halos = [
-        pltpu.make_async_remote_copy(
-            o.at[pl.ds(c.length, WINDOW), :], o.at[pl.ds(0, WINDOW), :],
-            c.halo_send.at[t], c.halo_recv.at[t], device_id=after, device_id_type=MESH,
-        )
-        for t, o in enumerate((c.k, c.v))
-    ]
-    for halo in halos:
-        halo.start()
     newton(c)
     renorm(c)
-    for p in range(peers):
-        arrived(2, p)
     for halo in halos:
         halo.wait()
     tiles = rows // (WINDOW // 2)
 
     def turn(step):
-        peer = flip_by(me, order_of(step, peers), peers)
+        peer = flip_by(me, jnp.where(step == 0, 0, order_of(step - 1, peers)), peers)
+        arrived(2, peer)
         attention(c, peer * tiles, tiles)
         fast_rows(c, peer * rows)
 

time: 128 us -> 124 us (0.969)
  Pallas kernels: 123 us -> 119 us
    pallas_call x1, Pallas kernels: 123 us -> 119 us  [body(): pl.pallas_call(functools.partial(kernel, tuple(scratch), sizes(length, wi...]
where the time goes in v4:
time: 124 us
  Pallas kernels  119 us (96%)
  local copies, waits for them, and re-layouts  3.77 us (3%)
    pallas_call x1, Pallas kernels, body(): pl.pallas_call(functools.partial(kernel, tuple(scratch), sizes(length, wi...  119 us
    unnamed x1, local copies, waits for them, and re-layouts  3.13 us

profile of v4, /device:TPU:0, one launch (start us, length us, event | category | flops | bytes accessed | tf_op | source)
XLA Modules:
  0.0 123.8 jit_solution(3100384352171752128)
XLA Ops:
  0.0 0.7 convert_bitcast_fusion
  0.7 0.6 broadcast_in_dim.2.r
  1.3 119.3 %layer.1 = bf16[256,4096]{1,0:T(8,128)(2,1)} custom-call(s32[4]{0:T(128)} %bounds.1, f32[8,1,512]{2,1,0:T(1,128)} %bitcast.3, bf16[256,4096]{1,0:T(8,128)(2,1)} %q.1, bf16[256,4096]{1,0:T(8,128)(2,1)} %k.1, bf16[256,4096]{1,0:T(8,128)(2,1)} %v.1, f32[8,8,256]{2,1,0:T(8,128)} %broadcast_in_dim.2.r, bf16[2,512,1024]{2,1,0:T(8,128)(2,1)} %gate_all.1, ...), custom_call_target="tpu_custom_call" | custom-call | tf_op jit(solution)/shard_map/layer/pallas_call | solution.py:480
  120.7 3.1 %copy.11 = bf16[256,4096]{1,0:T(8,128)(2,1)} copy(bf16[256,4096]{1,0:T(8,128)(2,1)} %layer.1) | data formatting | bytes 4194304
